TPU v7x, 256 devices: a whole 4x4x8 slice. The times are simulated.
256 devices in a mesh: blk: 64 (over z, x, core), rep: 4 (over y).
Axes of the slice: x: 4, y: 4, z: 8, core: 2. Of those that a mesh axis runs over, the one named last changes fastest.
Arguments:
- amplitudes: float32 [64, 64, 16, 512], P('blk', None, 'rep'), may hold values from -6 to 6
- cycle_integrals: float32 [32, 64, 64, 512], P('rep', None, 'blk'), may hold values from -0.09375 to 0.09375
- cross_integrals: float32 [32, 64, 64, 512], P('rep', None, 'blk'), may hold values from -0.09375 to 0.09375
- occ_energy: float32 [64], replicated, may hold values from -2 to -0.5
- vir_energy_a: float32 [32], replicated, may hold values from 0.2 to 3
- vir_energy_b: float32 [16], replicated, may hold values from 0.2 to 3
Outputs:
- update: float32 [64, 32, 16, 64], P('blk', 'rep')
- residual_rms: float32 [], replicated
All inputs are finite; a program needn't handle non-finite values.
Results may differ from a plain program's by a relative error of at most 0.0006.
Values sent between devices are 32-bit elements; how exact they have to be, the bound alone decides.
A program may use at most 64 MiB of HBM per device.

v0:
```python
import jax
import jax.numpy as jnp
from jax import lax
from jax.sharding import PartitionSpec as P


def per_device(
    amplitudes, cycle_integrals, cross_integrals, occ_energy, vir_energy_a, vir_energy_b
):
    highest = lax.Precision.HIGHEST
    whole = lax.all_gather(amplitudes, "rep", axis=2, tiled=True)
    moved = lax.all_to_all(whole, "blk", split_axis=1, concat_axis=0, tiled=True)
    crossed = jnp.swapaxes(moved, 0, 1)
    rows = amplitudes.shape[0]
    part = cycle_integrals
    cycle = lax.psum_scatter(
        jnp.einsum("aikc,kjbc->iabj", part, whole, precision=highest),
        "blk",
        scatter_dimension=0,
        tiled=True,
    )
    part = cross_integrals
    cross = lax.psum_scatter(
        jnp.einsum("aikc,kjbc->iabj", part, crossed, precision=highest),
        "blk",
        scatter_dimension=0,
        tiled=True,
    )
    residual = cycle + cross
    a_count = cycle_integrals.shape[0]
    occ_local = lax.dynamic_slice_in_dim(occ_energy, lax.axis_index("blk") * rows, rows, 0)
    vir_local = lax.dynamic_slice_in_dim(vir_energy_a, lax.axis_index("rep") * a_count, a_count, 0)
    denom = (
        occ_local[:, None, None, None]
        + occ_energy[None, None, None, :]
        - vir_local[None, :, None, None]
        - vir_energy_b[None, None, :, None]
    )
    update = residual / denom
    squares = lax.psum(jnp.sum(residual * residual), ("blk", "rep"))
    total_count = (
        occ_energy.shape[0] * occ_energy.shape[0] * vir_energy_a.shape[0] * vir_energy_b.shape[0]
    )
    residual_rms = jnp.sqrt(squares / total_count)
    return (update, residual_rms)


def solution(mesh):
    return jax.shard_map(
        per_device,
        mesh=mesh,
        in_specs=(
            P("blk", None, "rep", None),
            P("rep", None, "blk", None),
            P("rep", None, "blk", None),
            P(),
            P(),
            P(),
        ),
        out_specs=(P("blk", "rep", None, None), P()),
        check_vma=False,
    )
```

profile of v0, /device:TPU:1, one launch (start us, length us, event | category | flops | bytes accessed | tf_op | source)
XLA Modules:
  0.0 354.6 jit_solution(3494779001392865081)
XLA Ops:
  7.2 0.0 all-gather.2.cloned.1.call-start
  7.2 2.0 copy.9
  9.2 0.0 all-gather.2.cloned.1.call-update
  9.2 37.5 %all-gather.2.cloned.1.call-done = f32[1,64,16,512]{3,1,0,2:T(8,128)} async-done(((f32[1,64,4,512]{3,1,0,2:T(8,128)}), f32[1,64,16,512]{3,1,0,2:T(8,128)}) %all-gather.2.cloned.1.call-update) | async-done | bytes 2097168 | tf_op jit(solution)/shard_map/all_gather | solution.py:11
  46.8 4.2 %copy.11 = f32[1,64,16,512]{3,2,0,1:T(8,128)} copy(f32[1,64,16,512]{3,1,0,2:T(8,128)} %all-gather.2.cloned.1.call-done) | data formatting | bytes 4194304 | tf_op jit(solution)/shard_map/all_gather | solution.py:11
  50.9 11.3 %all-to-all-start = ((f32[1,64,16,512]{3,2,0,1:T(8,128)}), f32[1,64,16,512]{3,2,0,1:T(8,128)}, u32[]{:S(2)}, u32[]{:S(2)}) async-start(f32[1,64,16,512]{3,2,0,1:T(8,128)} %copy.11), calls=%async_computation | async-start | bytes 4194304 | tf_op jit(solution)/shard_map/all_to_all | solution.py:12
  62.2 0.0 reduce-scatter.4.cloned.1.call-start
  62.3 0.0 copy-done
  62.3 0.0 copy-done.1
  62.3 9.0 %fusion.1 = f32[64,16,8,64]{3,1,2,0:T(8,128)} fusion(f32[1,64,16,512]{3,1,0,2:T(8,128)S(1)} %copy-done, f32[8,64,1,512]{3,2,1,0:T(1,128)S(1)} %copy-done.1), kind=kOutput, calls=%fused_computation.2 | convolution fusion | flops 3221225472 | bytes 5242880 | tf_op jit(solution)/shard_map/aikc,kjbc->iabj/dot_general | solution.py:17
  71.3 40.6 %all-to-all-done = f32[1,64,16,512]{3,2,0,1:T(8,128)} async-done(((f32[1,64,16,512]{3,2,0,1:T(8,128)}), f32[1,64,16,512]{3,2,0,1:T(8,128)}, u32[]{:S(2)}, u32[]{:S(2)}) %all-to-all-start) | async-done | bytes 2097184 | tf_op jit(solution)/shard_map/all_to_all | solution.py:12
  111.9 10.5 %add_bitcast_fusion = f32[64,8,16,64]{0,2,1,3:T(8,128)} fusion(f32[64,16,8,64]{3,1,2,0:T(8,128)} %fusion.1, f32[1,64,16,512]{3,2,0,1:T(8,128)} %all-to-all-done, f32[8,64,1,512]{3,2,1,0:T(1,128)} %param.8), kind=kOutput, calls=%fused_computation | convolution fusion | flops 3221749760 | bytes 7340032 | tf_op jit(solution)/shard_map/aikc,kjbc->iabj/dot_general | solution.py:24
  122.4 6.1 %copy.12 = f32[64,8,16,64]{3,2,1,0:T(8,128)} copy(f32[64,8,16,64]{0,2,1,3:T(8,128)} %add_bitcast_fusion) | data formatting | bytes 4194304 | tf_op jit(solution)/shard_map/add | solution.py:29
  128.5 0.0 reduce-scatter.4.cloned.1.call-update
  128.5 0.6 copy-done.4
  129.1 0.6 dynamic_slice.6
  129.7 0.0 copy-done.3
  129.7 0.1 dynamic_slice.7
  129.8 0.6 broadcast_add_fusion
  130.4 0.1 broadcast_subtract_fusion
  130.5 133.6 %reduce-scatter.4.cloned.1.call-done = f32[1,8,16,64]{3,2,1,0:T(8,128)} async-done(((f32[64,8,16,64]{3,2,1,0:T(8,128)}), f32[1,8,16,64]{3,2,1,0:T(8,128)}) %reduce-scatter.4.cloned.1.call-update) | async-done | bytes 32784
  264.1 0.0 copy-done.2
  264.1 2.1 multiply_reduce_fusion
  266.2 79.7 %psum.7 = f32[]{:T(128)} all-reduce(f32[]{:T(128)} %get-tuple-element.4), channel_id=1, replica_groups=mesh['blk'=64,'rep'=4] {'blk','rep'}, use_global_device_ids=true, to_apply=%region_3.0 | all-reduce | flops 1 | bytes 8 | tf_op jit(solution)/shard_map/psum | solution.py:40
  (5 shorter events, 0.0 us)
Async XLA Ops:
  7.2 39.6 %all-gather.2.cloned.1.call-start = ((), (), s32[]{:S(2)}) async-start(), calls=%async_computation.2 | async-start | bytes 2621440 | tf_op jit(solution)/shard_map/all_gather | solution.py:11
  50.9 11.3 %copy-start = (f32[1,64,16,512]{3,1,0,2:T(8,128)S(1)}, f32[1,64,16,512]{3,1,0,2:T(8,128)}, u32[]{:S(2)}) copy-start(f32[1,64,16,512]{3,1,0,2:T(8,128)} %all-gather.2.cloned.1.call-done) | copy-start | bytes 6291460
  50.9 11.3 %copy-start.1 = (f32[8,64,1,512]{3,2,1,0:T(1,128)S(1)}, f32[8,64,1,512]{3,2,1,0:T(1,128)}, u32[]{:S(2)}) copy-start(f32[8,64,1,512]{3,2,1,0:T(1,128)} %param.7) | copy-start | bytes 3145732
  50.9 60.9 %all-to-all-start = ((f32[1,64,16,512]{3,2,0,1:T(8,128)}), f32[1,64,16,512]{3,2,0,1:T(8,128)}, u32[]{:S(2)}, u32[]{:S(2)}) async-start(f32[1,64,16,512]{3,2,0,1:T(8,128)} %copy.11), calls=%async_computation | async-start | bytes 4194304 | tf_op jit(solution)/shard_map/all_to_all | solution.py:12
  62.2 201.9 %reduce-scatter.4.cloned.1.call-start = ((), (), s32[]{:S(2)}) async-start(), calls=%async_computation.3 | async-start | bytes 4259840
  128.5 0.7 copy-start.4
  128.5 1.2 copy-start.3
  128.5 135.6 %copy-start.2 = (f32[16]{0:T(128)S(1)}, f32[16]{0:T(128)}, u32[]{:S(2)}) copy-start(f32[16]{0:T(128)} %param.11) | copy-start | bytes 196
Sparse Core Ops, SparseCore 0:
  9.8 36.9 all-gather.1
  128.6 135.4 reduce-scatter.3
where the time goes:
time: 355 us
  waiting for transfers between devices  212 us (60%)
  blocking collectives  79.7 us (22%)
  matrix products  19.5 us (5%)
  between operations  15.9 us (4%)
  local copies, waits for them, and re-layouts  13.5 us (4%)
  starting transfers between devices  11.4 us (3%)
    unnamed x3, waiting for transfers between devices  134 us
    psum x1, blocking collectives, per_device(): squares = lax.psum(jnp.sum(residual * residual), ('blk', 'rep'))  79.7 us
    all_to_all x1, waiting for transfers between devices, per_device(): lax.all_to_all(whole, 'blk', split_axis=1, concat_axis=0, tiled=True)  40.6 us
    all_gather x1, waiting for transfers between devices, per_device(): whole = lax.all_gather(amplitudes, 'rep', axis=2, tiled=True)  37.5 us
    all_to_all x1, starting transfers between devices, per_device(): lax.all_to_all(whole, 'blk', split_axis=1, concat_axis=0, tiled=True)  11.3 us
    dot_general x1, matrix products, per_device(): jnp.einsum('aikc,kjbc->iabj', part, crossed, precision=highest)  10.5 us
    dot_general x1, matrix products, per_device(): jnp.einsum('aikc,kjbc->iabj', part, whole, precision=highest)  8.97 us
  transfers between devices with their start and end apart: 3, of which 3 were waited for; matrix products, arithmetic and copies ran while one was open for 3% of the time, Pallas kernels for 0%

commit v1 on v0

--- a/solution.py
+++ b/solution.py
@@ -8,7 +8,9 @@
     amplitudes, cycle_integrals, cross_integrals, occ_energy, vir_energy_a, vir_energy_b
 ):
     highest = lax.Precision.HIGHEST
-    whole = lax.all_gather(amplitudes, "rep", axis=2, tiled=True)
+    whole = jnp.concatenate(
+        lax.all_to_all(jnp.stack([amplitudes] * lax.axis_size("rep")), "rep", 0, 0), axis=2
+    )
     moved = lax.all_to_all(whole, "blk", split_axis=1, concat_axis=0, tiled=True)
     crossed = jnp.swapaxes(moved, 0, 1)
     rows = amplitudes.shape[0]

time: 355 us -> 348 us (0.980)
  waiting for transfers between devices: 212 us -> 174 us
  blocking collectives: 79.7 us -> 110 us
    all_gather x1 -> x0, waiting for transfers between devices: 37.5 us -> none  [per_device(): whole = lax.all_gather(amplitudes, 'rep', axis=2, tiled=True)]
    all_to_all x0 -> x1, blocking collectives: none -> 30.3 us  [per_device(): lax.all_to_all(jnp.stack([amplitudes] * lax.axis_size('rep')), 'rep', 0, 0)]
    all_gather x1 -> x0, local copies, waits for them, and re-layouts: 4.16 us -> none  [per_device(): whole = lax.all_gather(amplitudes, 'rep', axis=2, tiled=True)]
    unnamed x3 -> x2, waiting for transfers between devices: 134 us -> 133 us
  transfers between devices with their start and end apart: 3 -> 2, of which waited for: 3 -> 2; matrix products, arithmetic and copies ran while one was open for 3% -> 3% of each run, Pallas kernels for 0% -> 0%
where the time goes in v1:
time: 348 us; the launch traced here: 347 us
  waiting for transfers between devices  174 us (50%)
  blocking collectives  110 us (32%)
  matrix products  19.5 us (6%)
  between operations  15.9 us (5%)
  starting transfers between devices  13.7 us (4%)
  local copies, waits for them, and re-layouts  11.9 us (3%)
    unnamed x2, waiting for transfers between devices  133 us
    psum x1, blocking collectives, per_device(): squares = lax.psum(jnp.sum(residual * residual), ('blk', 'rep'))  79.5 us
    all_to_all x1, waiting for transfers between devices, per_device(): lax.all_to_all(whole, 'blk', split_axis=1, concat_axis=0, tiled=True)  40.6 us
    all_to_all x1, blocking collectives, per_device(): lax.all_to_all(jnp.stack([amplitudes] * lax.axis_size('rep')), 'rep', 0, 0)  30.3 us
    all_to_all x1, starting transfers between devices, per_device(): lax.all_to_all(whole, 'blk', split_axis=1, concat_axis=0, tiled=True)  13.6 us
    dot_general x1, matrix products, per_device(): jnp.einsum('aikc,kjbc->iabj', part, crossed, precision=highest)  10.5 us
    dot_general x1, matrix products, per_device(): jnp.einsum('aikc,kjbc->iabj', part, whole, precision=highest)  8.96 us
  transfers between devices with their start and end apart: 2, of which 2 were waited for; matrix products, arithmetic and copies ran while one was open for 3% of the time, Pallas kernels for 0%

profile of v1, /device:TPU:1, one launch (start us, length us, event | category | flops | bytes accessed | tf_op | source)
XLA Modules:
  0.0 347.3 jit_solution(6238439928332378478)
XLA Ops:
  7.2 1.4 stack.2
  8.5 30.3 %all_to_all.14 = f32[4,1,64,4,512]{4,3,2,1,0:T(4,128)S(1)} all-to-all(f32[4,1,64,4,512]{4,3,2,1,0:T(4,128)S(1)} %stack.2), channel_id=1, replica_groups=mesh['blk'=64,'rep'=4] {'rep'}, dimensions={0} | all-to-all | bytes 4194304 | tf_op jit(solution)/shard_map/all_to_all | solution.py:12
  38.8 0.6 copy.11
  39.5 2.5 copy.13
  42.0 0.0 copy-start
  42.0 13.6 %all-to-all-start.1 = ((f32[1,64,16,512]{3,2,0,1:T(8,128)}), f32[1,64,16,512]{3,2,0,1:T(8,128)}, u32[]{:S(2)}, u32[]{:S(2)}) async-start(f32[1,64,16,512]{3,2,0,1:T(8,128)} %copy.13), calls=%async_computation.1 | async-start | bytes 4194304 | tf_op jit(solution)/shard_map/all_to_all | solution.py:14
  55.6 0.0 reduce-scatter.4.cloned.1.call-start
  55.6 0.0 copy-done
  55.7 9.0 %fusion.1 = f32[64,16,8,64]{3,1,2,0:T(8,128)} fusion(f32[64,16,512,1]{2,0,1,3:T(8,128)S(1)} %bitcast.25, f32[8,64,1,512]{3,2,1,0:T(1,128)S(1)} %copy-done), kind=kOutput, calls=%fused_computation.2 | convolution fusion | flops 3221225472 | bytes 5242880 | tf_op jit(solution)/shard_map/aikc,kjbc->iabj/dot_general | solution.py:19
  64.6 40.6 %all-to-all-done.1 = f32[1,64,16,512]{3,2,0,1:T(8,128)} async-done(((f32[1,64,16,512]{3,2,0,1:T(8,128)}), f32[1,64,16,512]{3,2,0,1:T(8,128)}, u32[]{:S(2)}, u32[]{:S(2)}) %all-to-all-start.1) | async-done | bytes 2097184 | tf_op jit(solution)/shard_map/all_to_all | solution.py:14
  105.2 10.5 %add_bitcast_fusion = f32[64,8,16,64]{0,2,1,3:T(8,128)} fusion(f32[64,16,8,64]{3,1,2,0:T(8,128)} %fusion.1, f32[1,64,16,512]{3,2,0,1:T(8,128)} %all-to-all-done.1, f32[8,64,1,512]{3,2,1,0:T(1,128)} %param.8), kind=kOutput, calls=%fused_computation | convolution fusion | flops 3221749760 | bytes 7340032 | tf_op jit(solution)/shard_map/aikc,kjbc->iabj/dot_general | solution.py:26
  115.7 6.1 %copy.14 = f32[64,8,16,64]{3,2,1,0:T(8,128)} copy(f32[64,8,16,64]{0,2,1,3:T(8,128)} %add_bitcast_fusion) | data formatting | bytes 4194304 | tf_op jit(solution)/shard_map/add | solution.py:31
  121.9 0.0 copy-start.3
  121.9 0.0 reduce-scatter.4.cloned.1.call-update
  121.9 0.6 copy-done.3
  122.5 0.6 dynamic_slice.6
  123.1 0.0 copy-done.2
  123.1 0.1 dynamic_slice.7
  123.2 0.6 broadcast_add_fusion
  123.8 0.1 broadcast_subtract_fusion
  123.9 133.1 %reduce-scatter.4.cloned.1.call-done = f32[1,8,16,64]{3,2,1,0:T(8,128)} async-done(((f32[64,8,16,64]{3,2,1,0:T(8,128)}), f32[1,8,16,64]{3,2,1,0:T(8,128)}) %reduce-scatter.4.cloned.1.call-update) | async-done | bytes 32784
  257.0 0.0 copy-done.1
  257.0 2.1 multiply_reduce_fusion
  259.1 79.5 %psum.7 = f32[]{:T(128)} all-reduce(f32[]{:T(128)} %get-tuple-element.4), channel_id=1, replica_groups=mesh['blk'=64,'rep'=4] {'blk','rep'}, use_global_device_ids=true, to_apply=%region_3.0 | all-reduce | flops 1 | bytes 8 | tf_op jit(solution)/shard_map/psum | solution.py:42
  (2 shorter events, 0.0 us)
Async XLA Ops:
  42.0 13.7 %copy-start = (f32[8,64,1,512]{3,2,1,0:T(1,128)S(1)}, f32[8,64,1,512]{3,2,1,0:T(1,128)}, u32[]{:S(2)}) copy-start(f32[8,64,1,512]{3,2,1,0:T(1,128)} %param.7) | copy-start | bytes 3145732
  42.0 63.2 %all-to-all-start.1 = ((f32[1,64,16,512]{3,2,0,1:T(8,128)}), f32[1,64,16,512]{3,2,0,1:T(8,128)}, u32[]{:S(2)}, u32[]{:S(2)}) async-start(f32[1,64,16,512]{3,2,0,1:T(8,128)} %copy.13), calls=%async_computation.1 | async-start | bytes 4194304 | tf_op jit(solution)/shard_map/all_to_all | solution.py:14
  55.6 201.4 %reduce-scatter.4.cloned.1.call-start = ((), (), s32[]{:S(2)}) async-start(), calls=%async_computation.3 | async-start | bytes 4259840
  121.9 0.7 copy-start.3
  121.9 1.2 copy-start.2
  121.9 135.1 %copy-start.1 = (f32[16]{0:T(128)S(1)}, f32[16]{0:T(128)}, u32[]{:S(2)}) copy-start(f32[16]{0:T(128)} %param.11) | copy-start | bytes 196
Sparse Core Ops, SparseCore 0:
  122.0 134.9 reduce-scatter.3
